TPU v7x, 256 devices: a whole 4x4x8 slice. The times are simulated.
256 devices in a mesh: ctx: 16 (over y, x_lo, core), rep: 8 (over z), head: 2 (over x_hi).
Axes of the slice: x: 4 (x_hi: 2, x_lo: 2; x = x_hi * 2 + x_lo), y: 4, z: 8, core: 2. Of those that a mesh axis runs over, the one named last changes fastest.
Arguments:
- inputs: bfloat16 [8, 8192, 2048], P('rep', 'ctx', 'head'), may hold values from -6 to 6
- queries: bfloat16 [8, 8192, 2048], P('rep', 'ctx', 'head'), may hold values from -6 to 6
- keys: bfloat16 [8, 8192, 2048], P('rep', 'ctx', 'head'), may hold values from -6 to 6
- targets: bfloat16 [8, 8192, 2048], P('rep', 'ctx', 'head'), may hold values from -3 to 3
- value_weight: bfloat16 [8, 2048, 2048], P('rep', None, 'head'), may hold values from -0.125 to 0.125
- anchor: float32 [2048, 2048], P('ctx', 'head'), may hold values from -0.125 to 0.125
- momentum: float32 [2048, 2048], P('ctx', 'head'), may hold values from -6 to 6
Outputs:
- anchor_next: float32 [8, 2048, 2048], P('rep', 'ctx', 'head')
- momentum_next: float32 [8, 2048, 2048], P('rep', 'ctx', 'head')
All inputs are finite; a program needn't handle non-finite values.
Results may differ from a plain program's by a relative error of at most 0.02.
Values may be sent and summed in bfloat16 or wider, within the bound.
A program may use at most 64 MiB of HBM per device.

v0:
```python
import math
import jax
import jax.numpy as jnp
from jax import lax
from jax.sharding import PartitionSpec as P

HEAD_DIM = 128
inner_rate = 0.05
slow_decay = 0.5
outer_rate = 1.0


def carried_in(shard, axis, join, neutral, backward):
    count = lax.axis_size(axis)
    place = lax.axis_index(axis)
    ahead = count - 1 - place if backward else place
    gathered = lax.all_gather(shard.astype(jnp.bfloat16), axis)
    state = jnp.zeros_like(shard) + jnp.asarray(neutral, shard.dtype)

    def one(turn, state):
        source = count - 1 - turn if backward else turn
        return join(state, lax.dynamic_index_in_dim(gathered, source, 0, False).astype(shard.dtype))

    return lax.fori_loop(0, ahead, one, state)


def from_partner(block, axis, apart):
    count = lax.axis_size(axis)
    route = []
    for low in range(count):
        high = low | 1 << apart
        if high != low and high < count:
            route += [(low, high), (high, low)]
    return lax.ppermute(block, axis, route)


def add_states(earlier, later):
    return earlier + later


def carried(local_state, forward):
    empty = jnp.zeros_like(local_state)
    if forward:
        return carried_in(local_state, "ctx", add_states, empty, False)
    return carried_in(local_state, "ctx", add_states, empty, True)


def mix_total(delta):
    for bit_number in range(2):
        delta = (
            delta + from_partner(delta.astype(jnp.bfloat16), "rep", bit_number).astype(delta.dtype)
        ) * 0.5
    return delta


def mix_rows(delta):
    return mix_total(delta)


def local(inputs, queries, keys, targets, value_weight, anchor, momentum):
    n_blocks = lax.axis_size("ctx")
    tokens_here = queries.shape[1]
    local_width = queries.shape[2]
    heads_here = local_width // HEAD_DIM
    sequence = tokens_here * n_blocks
    attn_scale = 1.0 / math.sqrt(HEAD_DIM * sequence)
    loss_scale = 1.0 / math.sqrt(sequence)
    weights_local = value_weight[0]
    model_width = weights_local.shape[0]
    share_rows = model_width // n_blocks
    first_row = lax.axis_index("ctx") * share_rows
    weight_rows = lax.dynamic_slice_in_dim(weights_local, first_row, share_rows, 0).astype(
        jnp.float32
    )
    drift = (anchor - weight_rows) / inner_rate
    features = lax.all_gather(inputs, "head", axis=2, tiled=True)[0]
    values = jnp.dot(features, weights_local, preferred_element_type=jnp.float32).astype(
        jnp.bfloat16
    )
    query_heads = queries[0].reshape(tokens_here, heads_here, HEAD_DIM)
    key_heads = keys[0].reshape(tokens_here, heads_here, HEAD_DIM)
    value_heads = values.reshape(tokens_here, heads_here, HEAD_DIM)
    target_heads = targets[0].reshape(tokens_here, heads_here, HEAD_DIM)
    scores = jnp.einsum("thd,shd->hts", query_heads, key_heads, preferred_element_type=jnp.float32)
    causal = jnp.arange(tokens_here)[:, None] >= jnp.arange(tokens_here)[None, :]
    weighted = jnp.where(causal[None], scores, 0.0).astype(jnp.bfloat16)
    local_state = jnp.einsum(
        "shd,she->hde", key_heads, value_heads, preferred_element_type=jnp.float32
    )
    prefix_state = carried(local_state, True)
    outputs = attn_scale * (
        jnp.einsum("hts,she->the", weighted, value_heads, preferred_element_type=jnp.float32)
        + jnp.einsum(
            "thd,hde->the",
            query_heads,
            prefix_state.astype(jnp.bfloat16),
            preferred_element_type=jnp.float32,
        )
    )
    grad_out = (loss_scale * (outputs - target_heads.astype(jnp.float32))).astype(jnp.bfloat16)
    back_local = jnp.einsum(
        "thd,the->hde", query_heads, grad_out, preferred_element_type=jnp.float32
    )
    suffix_state = carried(back_local, False)
    grad_values = attn_scale * (
        jnp.einsum("hts,the->she", weighted, grad_out, preferred_element_type=jnp.float32)
        + jnp.einsum(
            "shd,hde->she",
            key_heads,
            suffix_state.astype(jnp.bfloat16),
            preferred_element_type=jnp.float32,
        )
    )
    grad_values = grad_values.astype(jnp.bfloat16).reshape(tokens_here, local_width)
    gradient = lax.psum_scatter(
        lax.dot_general(
            features, grad_values, (((0,), (0,)), ((), ())), preferred_element_type=jnp.float32
        ).astype(jnp.bfloat16),
        "ctx",
        scatter_dimension=0,
        tiled=True,
    ).astype(jnp.float32)
    mixed = mix_rows(drift + gradient)
    momentum_next = slow_decay * momentum + mixed
    anchor_next = anchor - outer_rate * inner_rate * momentum_next
    return (anchor_next[None], momentum_next[None])


def solution(mesh):
    placed = (
        P("rep", "ctx", "head"),
        P("rep", "ctx", "head"),
        P("rep", "ctx", "head"),
        P("rep", "ctx", "head"),
        P("rep", None, "head"),
        P("ctx", "head"),
        P("ctx", "head"),
    )
    return jax.shard_map(
        local,
        mesh=mesh,
        in_specs=placed,
        out_specs=(P("rep", "ctx", "head"), P("rep", "ctx", "head")),
        check_vma=False,
    )
```

profile of v0, /device:TPU:27, one launch (start us, length us, event | category | flops | bytes accessed | tf_op | source)
XLA Modules:
  0.0 289.3 jit_solution(1893113426766698581)
XLA Ops:
  7.9 1.5 copy.54
  9.4 41.6 %all-gather.6.cloned.1.call-done = bf16[1,512,2048]{2,1,0:T(8,128)(2,1)} async-done(((bf16[1,512,1024]{2,1,0:T(8,128)(2,1)}), bf16[1,512,2048]{2,1,0:T(8,128)(2,1)}) %all-gather.6.cloned.1.call-update) | async-done | bytes 2097168 | tf_op jit(solution)/shard_map/all_gather | solution.py:76
  51.1 5.2 %fusion.6 = bf16[512,1024]{1,0:T(8,128)(2,1)S(1)} fusion(bf16[1,2048,1024]{2,1,0:T(8,128)(2,1)} %param.15, bf16[1,512,2048]{2,1,0:T(8,128)(2,1)} %all-gather.6.cloned.1.call-done), kind=kOutput, calls=%fused_computation.12 | convolution fusion | flops 2148007936 | bytes 7340032 | tf_op jit(solution)/shard_map/dot_general | solution.py:77
  58.2 1.5 copy.53
  59.7 3.0 %copy.38 = f32[1,512,1024]{1,2,0:T(8,128)} copy(bf16[1,512,1024]{2,1,0:T(8,128)(2,1)} %param.14) | data formatting | bytes 3145728 | tf_op jit(solution)/shard_map/convert_element_type | solution.py:100
  62.8 1.4 select_convert_fusion
  64.2 1.9 copy-done
  66.1 1.5 fusion.25
  67.6 29.8 %all-gather.8.cloned.1.call-done = bf16[128,128,128]{2,1,0:T(8,128)(2,1)} async-done(((bf16[8,128,128]{2,1,0:T(8,128)(2,1)}), bf16[128,128,128]{2,1,0:T(8,128)(2,1)}) %all-gather.8.cloned.1.call-update) | async-done | bytes 4194320 | tf_op jit(solution)/shard_map/all_gather | solution.py:17
  97.4 16.5 %while.22 = (s32[]{:T(128)}, f32[8,128,128]{2,1,0:T(8,128)S(1)}, s32[]{:T(128)}, bf16[16,8,128,128]{3,2,1,0:T(8,128)(2,1)}, s32[]{:T(128)}, /*index=5*/s32[]{:T(128)}, s32[]{:T(128)}) while((s32[]{:T(128)}, f32[8,128,128]{2,1,0:T(8,128)S(1)}, s32[]{:T(128)}, bf16[16,8,128,128]{3,2,1,0:T(8,128)(2,1)}, s32[]{:T(128)}, /*index=5*/s32[]{:T(128)}, ...), condition=%wide.region_1.2_spmd, body=%wide.region_0.1_spmd.sunk | while | flops 262149 | bytes 1310835 | solution.py:24
  97.4 1.1 convert_add_fusion.4
  98.5 1.1 convert_add_fusion.4
  100.7 1.1 convert_add_fusion.4
  101.8 1.1 convert_add_fusion.4
  102.9 1.1 convert_add_fusion.4
  106.2 1.1 convert_add_fusion.4
  107.3 1.1 convert_add_fusion.4
  108.4 1.1 convert_add_fusion.4
  111.7 1.1 convert_add_fusion.4
  112.8 1.1 convert_add_fusion.4
  113.9 2.6 fusion.3
  118.9 3.2 %fusion.26 = f32[8,128,512]{2,1,0:T(8,128)S(1)} fusion(bf16[512,8,128]{0,2,1:T(8,128)(2,1)} %copy-done.1, bf16[8,512,512]{2,1,0:T(8,128)(2,1)} %copy-done), kind=kOutput, calls=%fused_computation.37 | convolution fusion | flops 536870912 | bytes 7340032 | tf_op jit(solution)/shard_map/hts,the->she/dot_general | solution.py:106
  122.1 35.7 %all-gather.10.cloned.1.call-done = bf16[128,128,128]{2,1,0:T(8,128)(2,1)} async-done(((bf16[8,128,128]{2,1,0:T(8,128)(2,1)}), bf16[128,128,128]{2,1,0:T(8,128)(2,1)}) %all-gather.10.cloned.1.call-update) | async-done | bytes 4194320 | tf_op jit(solution)/shard_map/all_gather | solution.py:17
  157.9 1.9 multiply_convert_fusion
  159.8 4.3 %convert_bitcast_fusion = bf16[2048,1024]{0,1:T(8,128)(2,1)} fusion(bf16[512,1024]{0,1:T(8,128)(2,1)S(1)} %bitcast.81, bf16[1,512,2048]{2,1,0:T(8,128)(2,1)S(1)} %copy-done.7), kind=kOutput, calls=%fused_computation.5 | convolution fusion | flops 2149580800 | bytes 7340032 | tf_op jit(solution)/shard_map/dot_general | solution.py:116
  164.2 6.4 %copy.49 = bf16[2048,1024]{1,0:T(8,128)(2,1)} copy(bf16[2048,1024]{0,1:T(8,128)(2,1)} %convert_bitcast_fusion) | data formatting | bytes 8388608
  172.0 86.7 %reduce-scatter.4.cloned.1.call-done = bf16[128,1024]{1,0:T(8,128)(2,1)} async-done(((bf16[2048,1024]{1,0:T(8,128)(2,1)}), bf16[128,1024]{1,0:T(8,128)(2,1)}) %reduce-scatter.4.cloned.1.call-update) | async-done | bytes 262160
  258.7 1.1 copy.50
  259.9 1.4 collective-permute-start
  261.3 5.0 %collective-permute-done = bf16[128,1024]{0,1:T(8,128)(2,1)S(1)} collective-permute-done((bf16[128,1024]{0,1:T(8,128)(2,1)S(1)}, bf16[128,1024]{0,1:T(8,128)(2,1)S(1)}, u32[]{:S(2)}, u32[]{:S(2)}) %collective-permute-start) | collective-permute-done | bytes 262176 | tf_op jit(solution)/shard_map/ppermute | solution.py:34
  266.5 2.4 collective-permute-start.1
  269.1 11.4 %collective-permute-done.1 = bf16[128,1024]{0,1:T(8,128)(2,1)S(1)} collective-permute-done((bf16[128,1024]{0,1:T(8,128)(2,1)S(1)}, bf16[128,1024]{0,1:T(8,128)(2,1)S(1)}, u32[]{:S(2)}, u32[]{:S(2)}) %collective-permute-start.1) | collective-permute-done | bytes 262176 | tf_op jit(solution)/shard_map/ppermute | solution.py:34
  (46 shorter events, 14.7 us)
Async XLA Ops:
  7.2 43.9 %all-gather.6.cloned.1.call-start = ((), (), s32[]{:S(2)}) async-start(), calls=%async_computation.1 | async-start | bytes 3145728 | tf_op jit(solution)/shard_map/all_gather | solution.py:76
  7.9 89.5 %all-gather.8.cloned.1.call-start = ((), (), s32[]{:S(2)}) async-start(), calls=%async_computation.2 | async-start | bytes 4456448 | tf_op jit(solution)/shard_map/all_gather | solution.py:17
  9.4 53.3 %copy-start.2 = (bf16[64,8,8,128]{3,2,1,0:T(8,128)(2,1)}, bf16[64,8,8,128]{3,2,1,0:T(8,128)(2,1)S(1)}, u32[]{:S(2)}) copy-start(bf16[64,8,8,128]{3,2,1,0:T(8,128)(2,1)S(1)} %copy.54) | copy-start | bytes 3145732
  58.1 99.7 %all-gather.10.cloned.1.call-start = ((), (), s32[]{:S(2)}) async-start(), calls=%async_computation.3 | async-start | bytes 4456448 | tf_op jit(solution)/shard_map/all_gather | solution.py:17
  59.7 3.1 %copy-start.3 = (bf16[64,8,8,128]{3,2,1,0:T(8,128)(2,1)}, bf16[64,8,8,128]{3,2,1,0:T(8,128)(2,1)S(1)}, u32[]{:S(2)}) copy-start(bf16[64,8,8,128]{3,2,1,0:T(8,128)(2,1)S(1)} %copy.53) | copy-start | bytes 3145732
  64.2 1.9 copy-start
  113.9 3.6 %copy-start.4 = (bf16[64,8,8,128]{3,2,1,0:T(8,128)(2,1)S(1)}, bf16[64,8,8,128]{3,2,1,0:T(8,128)(2,1)}, u32[]{:S(2)}) copy-start(bf16[64,8,8,128]{3,2,1,0:T(8,128)(2,1)} %copy-done.3) | copy-start | bytes 3145732
  116.5 1.0 copy-start.1
  118.9 139.8 %reduce-scatter.4.cloned.1.call-start = ((), (), s32[]{:S(2)}) async-start(), calls=%async_computation.4 | async-start | bytes 4456448
  157.9 1.9 copy-start.7
  170.6 1.2 copy-start.5
  171.8 97.1 %copy-start.6 = (f32[128,1024]{1,0:T(8,128)S(1)}, f32[128,1024]{1,0:T(8,128)}, u32[]{:S(2)}) copy-start(f32[128,1024]{1,0:T(8,128)} %param.17) | copy-start | bytes 1572868
  259.9 6.4 %collective-permute-start = (bf16[128,1024]{0,1:T(8,128)(2,1)S(1)}, bf16[128,1024]{0,1:T(8,128)(2,1)S(1)}, u32[]{:S(2)}, u32[]{:S(2)}) collective-permute-start(bf16[128,1024]{0,1:T(8,128)(2,1)S(1)} %fusion.24), channel_id=1, source_target_pairs={{0,2},{2,0},{4,6},{6,4},{8,10},{10,8},{12,14},{14,12},{1,3},{3,1},... | collective-permute-start | bytes 786440 | tf_op jit(solution)/shard_map/ppermute | solution.py:34
  266.5 14.0 %collective-permute-start.1 = (bf16[128,1024]{0,1:T(8,128)(2,1)S(1)}, bf16[128,1024]{0,1:T(8,128)(2,1)S(1)}, u32[]{:S(2)}, u32[]{:S(2)}) collective-permute-start(bf16[128,1024]{0,1:T(8,128)(2,1)S(1)} %fusion.21), channel_id=1, source_target_pairs={{0,4},{4,0},{2,6},{6,2},{8,12},{12,8},{10,14},{14,10},{1,5},{5,1},... | collective-permute-start | bytes 786440 | tf_op jit(solution)/shard_map/ppermute | solution.py:34
Sparse Core Ops, SparseCore 0:
  9.8 41.2 all-gather.5
  58.3 39.0 all-gather.7
  119.0 38.7 all-gather.9
  170.7 87.9 reduce-scatter.3
where the time goes:
time: 290 us; the launch traced here: 289 us
  waiting for transfers between devices  211 us (73%)
  local copies, waits for them, and re-layouts  22.3 us (8%)
  matrix products  21 us (7%)
  other arithmetic  16.6 us (6%)
  between operations  14 us (5%)
  starting transfers between devices  3.93 us (1%)
    unnamed x5, waiting for transfers between devices  87.4 us
    all_gather x2, waiting for transfers between devices, carried_in(): gathered = lax.all_gather(shard.astype(jnp.bfloat16), axis)  65.5 us
    all_gather x1, waiting for transfers between devices, local(): features = lax.all_gather(inputs, 'head', axis=2, tiled=True)[0]  41.6 us
    ppermute x2, waiting for transfers between devices, from_partner(): return lax.ppermute(block, axis, route)  16.4 us
    add x15, other arithmetic, add_states(): return earlier + later  16 us
    unnamed x25, local copies, waits for them, and re-layouts  16 us
  transfers between devices with their start and end apart: 6, of which 6 were waited for; matrix products, arithmetic and copies ran while one was open for 5% of the time, Pallas kernels for 0%

commit v1 on v0

--- a/solution.py
+++ b/solution.py
@@ -73,7 +73,9 @@
         jnp.float32
     )
     drift = (anchor - weight_rows) / inner_rate
-    features = lax.all_gather(inputs, "head", axis=2, tiled=True)[0]
+    features = jnp.concatenate(
+        lax.all_to_all(jnp.stack([inputs] * lax.axis_size("head")), "head", 0, 0), axis=2
+    )[0]
     values = jnp.dot(features, weights_local, preferred_element_type=jnp.float32).astype(
         jnp.bfloat16
     )

time: 290 us -> 275 us (0.948)
  waiting for transfers between devices: 211 us -> 196 us
  local copies, waits for them, and re-layouts: 22.3 us -> 15 us
  starting transfers between devices: 3.93 us -> 7.6 us
  other arithmetic: 16.6 us -> 20 us
    reduce_scatter x0 -> x1, waiting for transfers between devices: none -> 88 us  [local(): lax.psum_scatter(lax.dot_general(features, grad_values, (((0,), (0,)), ((...]
    unnamed x5 -> x3, waiting for transfers between devices: 87.4 us -> 0.05 us
    all_gather x1 -> x0, waiting for transfers between devices: 41.6 us -> none  [local(): features = lax.all_gather(inputs, 'head', axis=2, tiled=True)[0]]
    all_to_all x0 -> x1, waiting for transfers between devices: none -> 24.2 us  [local(): lax.all_to_all(jnp.stack([inputs] * lax.axis_size('head')), 'head', 0, 0)]
    unnamed x25 -> x21, local copies, waits for them, and re-layouts: 16 us -> 8.8 us
    all_to_all x0 -> x1, starting transfers between devices: none -> 3.76 us  [local(): lax.all_to_all(jnp.stack([inputs] * lax.axis_size('head')), 'head', 0, 0)]
  transfers between devices with their start and end apart: 6 -> 6, of which waited for: 6 -> 6; matrix products, arithmetic and copies ran while one was open for 5% -> 4% of each run, Pallas kernels for 0% -> 0%
where the time goes in v1:
time: 275 us; the launch traced here: 274 us
  waiting for transfers between devices  196 us (71%)
  matrix products  21.4 us (8%)
  other arithmetic  20 us (7%)
  local copies, waits for them, and re-layouts  15 us (5%)
  between operations  14 us (5%)
  starting transfers between devices  7.6 us (3%)
    reduce_scatter x1, waiting for transfers between devices, local(): lax.psum_scatter(lax.dot_general(features, grad_values, (((0,), (0,)), ((...  88 us
    all_gather x2, waiting for transfers between devices, carried_in(): gathered = lax.all_gather(shard.astype(jnp.bfloat16), axis)  67 us
    all_to_all x1, waiting for transfers between devices, local(): lax.all_to_all(jnp.stack([inputs] * lax.axis_size('head')), 'head', 0, 0)  24.2 us
    ppermute x2, waiting for transfers between devices, from_partner(): return lax.ppermute(block, axis, route)  16.9 us
    add x15, other arithmetic, add_states(): return earlier + later  16 us
    unnamed x21, local copies, waits for them, and re-layouts  8.8 us
    dot_general x1, matrix products, local(): jnp.dot(features, weights_local, preferred_element_type=jnp.float32)  5.51 us
  transfers between devices with their start and end apart: 6, of which 6 were waited for; matrix products, arithmetic and copies ran while one was open for 4% of the time, Pallas kernels for 0%

profile of v1, /device:TPU:27, one launch (start us, length us, event | category | flops | bytes accessed | tf_op | source)
XLA Modules:
  0.0 274.4 jit_solution(2002932009475033674)
XLA Ops:
  7.2 1.5 copy.36
  8.7 1.5 pad_maximum_fusion
  10.2 3.8 %all-to-all-start = ((bf16[2,1,512,1024]{2,3,1,0:T(8,128)(2,1)}), bf16[2,1,512,1024]{2,3,1,0:T(8,128)(2,1)S(1)}, u32[]{:S(2)}, u32[]{:S(2)}) async-start(bf16[2,1,512,1024]{2,3,1,0:T(8,128)(2,1)} %pad_maximum_fusion), calls=%async_computation | async-start | bytes 4194304 | tf_op jit(solution)/shard_map/all_to_all | solution.py:77
  14.0 1.5 copy.55
  15.5 24.2 %all-to-all-done = bf16[2,1,512,1024]{2,3,1,0:T(8,128)(2,1)S(1)} async-done(((bf16[2,1,512,1024]{2,3,1,0:T(8,128)(2,1)}), bf16[2,1,512,1024]{2,3,1,0:T(8,128)(2,1)S(1)}, u32[]{:S(2)}, u32[]{:S(2)}) %all-to-all-start) | async-done | bytes 2097184 | tf_op jit(solution)/shard_map/all_to_all | solution.py:77
  39.7 1.4 copy-done.5
  41.1 5.5 %fusion.4 = bf16[512,1024]{1,0:T(8,128)(2,1)} fusion(bf16[512,2048]{0,1:T(8,128)(2,1)S(1)} %bitcast.71, bf16[1,2048,1024]{2,1,0:T(8,128)(2,1)} %param.15), kind=kOutput, calls=%fused_computation.11 | convolution fusion | flops 2148007936 | bytes 7340032 | tf_op jit(solution)/shard_map/dot_general | solution.py:79
  46.6 1.5 copy.53
  49.5 1.5 copy.54
  51.0 3.0 %copy.46 = f32[1,512,1024]{1,2,0:T(8,128)} copy(bf16[1,512,1024]{2,1,0:T(8,128)(2,1)} %param.14) | data formatting | bytes 3145728 | tf_op jit(solution)/shard_map/convert_element_type | solution.py:102
  54.1 1.4 select_convert_fusion
  55.5 1.9 copy-done
  57.4 1.5 fusion.22
  58.9 31.3 %all-gather.5.cloned.1.call-done = bf16[128,128,128]{2,1,0:T(8,128)(2,1)} async-done(((bf16[8,128,128]{2,1,0:T(8,128)(2,1)}), bf16[128,128,128]{2,1,0:T(8,128)(2,1)}) %all-gather.5.cloned.1.call-update) | async-done | bytes 4194320 | tf_op jit(solution)/shard_map/all_gather | solution.py:17
  90.2 16.4 %while.22 = (s32[]{:T(128)}, f32[8,128,128]{2,1,0:T(8,128)S(1)}, s32[]{:T(128)}, bf16[16,8,128,128]{3,2,1,0:T(8,128)(2,1)}, s32[]{:T(128)}, /*index=5*/s32[]{:T(128)}, s32[]{:T(128)}) while((s32[]{:T(128)}, f32[8,128,128]{2,1,0:T(8,128)S(1)}, s32[]{:T(128)}, bf16[16,8,128,128]{3,2,1,0:T(8,128)(2,1)}, s32[]{:T(128)}, /*index=5*/s32[]{:T(128)}, ...), condition=%wide.region_1.2_spmd, body=%wide.region_0.1_spmd.sunk | while | flops 262149 | bytes 1310843 | solution.py:24
  90.2 1.1 convert_add_fusion.4
  91.3 1.1 convert_add_fusion.4
  92.4 1.1 convert_add_fusion.4
  93.5 1.1 convert_add_fusion.4
  94.6 1.1 convert_add_fusion.4
  106.6 2.6 fusion.3
  111.6 3.2 %fusion.23 = f32[8,128,512]{2,1,0:T(8,128)S(1)} fusion(bf16[512,8,128]{0,2,1:T(8,128)(2,1)} %copy-done.1, bf16[8,512,512]{2,1,0:T(8,128)(2,1)} %copy-done), kind=kOutput, calls=%fused_computation.35 | convolution fusion | flops 536870912 | bytes 7340032 | tf_op jit(solution)/shard_map/hts,the->she/dot_general | solution.py:108
  114.8 35.7 %all-gather.7.cloned.1.call-done = bf16[128,128,128]{2,1,0:T(8,128)(2,1)} async-done(((bf16[8,128,128]{2,1,0:T(8,128)(2,1)}), bf16[128,128,128]{2,1,0:T(8,128)(2,1)}) %all-gather.7.cloned.1.call-update) | async-done | bytes 4194320 | tf_op jit(solution)/shard_map/all_gather | solution.py:17
  150.6 1.9 multiply_convert_fusion
  152.5 4.3 %convolution_convert_fusion = bf16[2048,1024]{1,0:T(8,128)(2,1)} fusion(bf16[512,2048]{0,1:T(8,128)(2,1)S(1)} %bitcast.72, bf16[512,1024]{0,1:T(8,128)(2,1)S(1)} %bitcast.75), kind=kOutput, calls=%fused_computation.5 | convolution fusion | flops 2149580800 | bytes 7340032 | tf_op jit(solution)/shard_map/dot_general | solution.py:118
  156.9 88.0 %reduce-scatter.2.cloned.1.call-done = bf16[128,1024]{1,0:T(8,128)(2,1)} async-done(((bf16[2048,1024]{1,0:T(8,128)(2,1)}), bf16[128,1024]{1,0:T(8,128)(2,1)}) %reduce-scatter.2.cloned.1.call-update) | async-done | bytes 262160 | tf_op jit(solution)/shard_map/reduce_scatter | solution.py:117
  244.9 1.1 fusion.20
  246.0 1.5 collective-permute-start
  247.6 4.9 %collective-permute-done = bf16[128,1024]{1,0:T(8,128)(2,1)S(1)} collective-permute-done((bf16[128,1024]{1,0:T(8,128)(2,1)S(1)}, bf16[128,1024]{1,0:T(8,128)(2,1)S(1)}, u32[]{:S(2)}, u32[]{:S(2)}) %collective-permute-start) | collective-permute-done | bytes 262176 | tf_op jit(solution)/shard_map/ppermute | solution.py:34
  252.6 2.2 collective-permute-start.1
  254.7 11.9 %collective-permute-done.1 = bf16[128,1024]{1,0:T(8,128)(2,1)S(1)} collective-permute-done((bf16[128,1024]{1,0:T(8,128)(2,1)S(1)}, bf16[128,1024]{1,0:T(8,128)(2,1)S(1)}, u32[]{:S(2)}, u32[]{:S(2)}) %collective-permute-start.1) | collective-permute-done | bytes 262176 | tf_op jit(solution)/shard_map/ppermute | solution.py:34
  266.7 1.1 multiply_bitcast_fusion
  (41 shorter events, 14.7 us)
Async XLA Ops:
  10.2 29.5 %all-to-all-start = ((bf16[2,1,512,1024]{2,3,1,0:T(8,128)(2,1)}), bf16[2,1,512,1024]{2,3,1,0:T(8,128)(2,1)S(1)}, u32[]{:S(2)}, u32[]{:S(2)}) async-start(bf16[2,1,512,1024]{2,3,1,0:T(8,128)(2,1)} %pad_maximum_fusion), calls=%async_computation | async-start | bytes 4194304 | tf_op jit(solution)/shard_map/all_to_all | solution.py:77
  13.9 76.2 %all-gather.5.cloned.1.call-start = ((), (), s32[]{:S(2)}) async-start(), calls=%async_computation.3 | async-start | bytes 4456448 | tf_op jit(solution)/shard_map/all_gather | solution.py:17
  15.5 38.6 %copy-start.2 = (bf16[64,8,8,128]{3,2,1,0:T(8,128)(2,1)}, bf16[64,8,8,128]{3,2,1,0:T(8,128)(2,1)S(1)}, u32[]{:S(2)}) copy-start(bf16[64,8,8,128]{3,2,1,0:T(8,128)(2,1)S(1)} %copy.55) | copy-start | bytes 3145732
  39.7 1.4 copy-start.5
  49.4 101.1 %all-gather.7.cloned.1.call-start = ((), (), s32[]{:S(2)}) async-start(), calls=%async_computation.4 | async-start | bytes 4456448 | tf_op jit(solution)/shard_map/all_gather | solution.py:17
  51.0 3.1 %copy-start.3 = (bf16[64,8,8,128]{3,2,1,0:T(8,128)(2,1)}, bf16[64,8,8,128]{3,2,1,0:T(8,128)(2,1)S(1)}, u32[]{:S(2)}) copy-start(bf16[64,8,8,128]{3,2,1,0:T(8,128)(2,1)S(1)} %copy.54) | copy-start | bytes 3145732
  55.4 1.9 copy-start
  106.6 3.6 %copy-start.4 = (bf16[64,8,8,128]{3,2,1,0:T(8,128)(2,1)S(1)}, bf16[64,8,8,128]{3,2,1,0:T(8,128)(2,1)}, u32[]{:S(2)}) copy-start(bf16[64,8,8,128]{3,2,1,0:T(8,128)(2,1)} %copy-done.3) | copy-start | bytes 3145732
  109.2 1.0 copy-start.1
  111.6 133.3 %reduce-scatter.2.cloned.1.call-start = ((), (), s32[]{:S(2)}) async-start(), calls=%async_computation.2 | async-start | bytes 4456448 | tf_op jit(solution)/shard_map/reduce_scatter | solution.py:117
  150.6 1.9 copy-start.6
  156.8 88.0 %copy-start.7 = (f32[128,1024]{1,0:T(8,128)S(1)}, f32[128,1024]{1,0:T(8,128)}, u32[]{:S(2)}) copy-start(f32[128,1024]{1,0:T(8,128)} %param.16) | copy-start | bytes 1572868
  156.9 109.8 %copy-start.8 = (f32[128,1024]{1,0:T(8,128)S(1)}, f32[128,1024]{1,0:T(8,128)}, u32[]{:S(2)}) copy-start(f32[128,1024]{1,0:T(8,128)} %param.17) | copy-start | bytes 1572868
  246.0 6.5 %collective-permute-start = (bf16[128,1024]{1,0:T(8,128)(2,1)S(1)}, bf16[128,1024]{1,0:T(8,128)(2,1)S(1)}, u32[]{:S(2)}, u32[]{:S(2)}) collective-permute-start(bf16[128,1024]{1,0:T(8,128)(2,1)S(1)} %get-tuple-element.115), channel_id=1, source_target_pairs={{0,2},{2,0},{4,6},{6,4},{8,10},{10,8},{12,14},{14,12},{1,3},{3,1},... | collective-permute-start | bytes 786440 | tf_op jit(solution)/shard_map/ppermute | solution.py:34
  252.6 14.1 %collective-permute-start.1 = (bf16[128,1024]{1,0:T(8,128)(2,1)S(1)}, bf16[128,1024]{1,0:T(8,128)(2,1)S(1)}, u32[]{:S(2)}, u32[]{:S(2)}) collective-permute-start(bf16[128,1024]{1,0:T(8,128)(2,1)S(1)} %fusion.17), channel_id=1, source_target_pairs={{0,4},{4,0},{2,6},{6,2},{8,12},{12,8},{10,14},{14,10},{1,5},{5,1},... | collective-permute-start | bytes 786440 | tf_op jit(solution)/shard_map/ppermute | solution.py:34
Sparse Core Ops, SparseCore 0:
  49.6 40.5 all-gather.4
  111.7 38.7 all-gather.6
  157.0 87.8 reduce-scatter.1
